TPU v7x, 512 devices: a whole 4x8x8 slice. The times are simulated.
512 devices in a mesh: ctx: 64 (over x, z, core), head: 8 (over y).
Axes of the slice: x: 4, y: 8, z: 8, core: 2. Of those that a mesh axis runs over, the one named last changes fastest.
Arguments:
- dec_states: bfloat16 [16384, 4096], P('ctx', 'head'), may hold values from -512 to 512
- norm_gain: float32 [4096], replicated, may hold values from 0.1 to 1.9
- w_query: bfloat16 [4096, 4096], P('ctx', 'head'), may hold values from -0.09375 to 0.09375
- enc_keys: bfloat16 [131072, 4096], P('ctx', 'head'), may hold values from -128 to 128
- enc_values: bfloat16 [131072, 4096], P('ctx', 'head'), may hold values from -24 to 24
- w_out: bfloat16 [4096, 4096], P('ctx', 'head'), may hold values from -0.09375 to 0.09375
- tgt_lengths: int32 [32], replicated, may hold values from 1 to 512, 8192 in all
- src_lengths: int32 [32], replicated, may hold values from 2049 to 4096, as said below
Outputs:
- attn_output: bfloat16 [16384, 4096], P('ctx', 'head')
Inputs may be any that keep to these rules, and one draw needn't show every extreme that they name: `tgt_lengths`: the lengths sum to 8192, and the longest equals 512. `src_lengths`: every example has more than 2048 encoder rows, and some example has all 4096.
All inputs are finite; a program needn't handle non-finite values.
Results may differ from a plain program's by a relative error of at most 0.009.
Values may be sent and summed in bfloat16 or wider, within the bound.
No kernel may reach another device: no remote copies, remote signals or barrier semaphores. Data moves between devices by JAX's collectives and lax.ppermute only.
A program may use at most 64 MiB of HBM per device.

v0:
```python
import jax
import jax.numpy as jnp
from jax import lax
from jax.sharding import PartitionSpec as P

DK = 64


def partner(value, axis, distance):
    mask = 2**distance
    pairs = [(source, source ^ mask) for source in range(lax.axis_size(axis))]
    return lax.ppermute(value, axis, pairs)


def attend(queries, keys, values, key_valid):
    row_count = queries.shape[0]
    head_count = queries.shape[1] // DK
    query_heads = jnp.moveaxis(queries.reshape(row_count, head_count, DK), 1, 0)
    key_heads = jnp.moveaxis(keys.reshape(-1, head_count, DK), 1, 0)
    value_heads = jnp.moveaxis(values.reshape(-1, head_count, DK), 1, 0)

    def one_head(head_items):
        query_head, key_head, value_head = head_items
        scores = jnp.dot(query_head, key_head.T, preferred_element_type=jnp.float32)
        scores = jnp.where(key_valid[None, :], scores, -jnp.inf)
        top_score = jnp.max(scores, axis=1)
        weights = jnp.exp(scores - top_score[:, None]).astype(jnp.bfloat16)
        totals = jnp.sum(weights.astype(jnp.float32), axis=1)
        weighted = jnp.dot(weights, value_head, preferred_element_type=jnp.float32)
        return (top_score, totals, weighted)

    top_score, totals, weighted = lax.map(one_head, (query_heads, key_heads, value_heads))
    return (top_score.T, totals.T, jnp.moveaxis(weighted, 0, 1).reshape(row_count, head_count * DK))


def combine_halves(first, second):
    top_one, totals_one, weighted_one = first
    top_two, totals_two, weighted_two = second
    row_count = weighted_one.shape[0]
    head_count = top_one.shape[1]
    largest = jnp.maximum(top_one, top_two)
    scale_one = jnp.exp(top_one - largest)
    scale_two = jnp.exp(top_two - largest)
    numer = (
        weighted_one.reshape(row_count, head_count, DK) * scale_one[:, :, None]
        + weighted_two.reshape(row_count, head_count, DK) * scale_two[:, :, None]
    )
    denom = totals_one * scale_one + totals_two * scale_two
    return (numer / denom[:, :, None]).reshape(row_count, head_count * DK)


def local(dec_states, norm_gain, w_query, enc_keys, enc_values, w_out, tgt_lengths, src_lengths):
    position = lax.axis_index("ctx")
    half_index = position % 2
    example = position // 2
    slot_ids = jnp.arange(tgt_lengths.shape[0], dtype=jnp.int32)
    tgt_len = jnp.sum(jnp.where(slot_ids == example, tgt_lengths, 0))
    src_len = jnp.sum(jnp.where(slot_ids == example, src_lengths, 0))
    enc_count = enc_keys.shape[0]
    full_states = lax.all_gather(dec_states, "head", axis=1, tiled=True)
    row_count = full_states.shape[0]
    states = full_states.astype(jnp.float32)
    normed = (
        states * lax.rsqrt(jnp.mean(states * states, axis=-1, keepdims=True) + 1e-06) * norm_gain
    ).astype(jnp.bfloat16)
    columns = normed
    queries = jnp.dot(
        columns,
        lax.all_gather(w_query, "ctx", axis=0, tiled=True),
        preferred_element_type=jnp.float32,
    ).astype(jnp.bfloat16)
    offsets = jnp.arange(enc_count, dtype=jnp.int32)
    own_valid = half_index * enc_count + offsets < src_len
    far_valid = (1 - half_index) * enc_count + offsets < src_len
    far_keys, far_values = partner((enc_keys, enc_values), "ctx", 0)
    nearby = attend(queries, enc_keys, enc_values, own_valid)
    distant = attend(queries, far_keys, far_values, far_valid)
    attended = combine_halves(nearby, distant)
    live_rows = half_index * row_count + jnp.arange(row_count, dtype=jnp.int32) < tgt_len
    attended = jnp.where(live_rows[:, None], attended, 0.0).astype(jnp.bfloat16)
    all_heads = lax.all_gather(attended, "head", axis=1, tiled=True)
    columns = all_heads
    projected = jnp.dot(
        columns,
        lax.all_gather(w_out, "ctx", axis=0, tiled=True),
        preferred_element_type=jnp.float32,
    )
    return projected.astype(jnp.bfloat16)


def solution(mesh):
    placed = (
        P("ctx", "head"),
        P(),
        P("ctx", "head"),
        P("ctx", "head"),
        P("ctx", "head"),
        P("ctx", "head"),
        P(),
        P(),
    )
    return jax.shard_map(
        local, mesh=mesh, in_specs=placed, out_specs=P("ctx", "head"), check_vma=False
    )
```

profile of v0, /device:TPU:2, one launch (start us, length us, event | category | flops | bytes accessed | tf_op | source)
XLA Modules:
  0.0 284.5 jit_solution(14177036345322470178)
XLA Ops:
  8.1 2.9 %copy.11 = bf16[2048,512]{0,1:T(8,128)(2,1)S(1)} copy(bf16[2048,512]{1,0:T(8,128)(2,1)} %param.15) | data formatting | bytes 4194304 | tf_op args[3]
  11.0 1.9 collective-permute-start
  12.9 4.0 %copy.12 = bf16[2048,512]{0,1:T(8,128)(2,1)} copy(bf16[2048,512]{1,0:T(8,128)(2,1)} %param.16) | data formatting | bytes 4194304 | tf_op args[4]
  16.9 2.5 collective-permute-start.1
  21.5 36.2 %all-gather.5.cloned.1.call-done = bf16[256,4096]{1,0:T(8,128)(2,1)} async-done(((bf16[256,512]{1,0:T(8,128)(2,1)}), bf16[256,4096]{1,0:T(8,128)(2,1)}) %all-gather.5.cloned.1.call-update) | async-done | bytes 2097168 | tf_op jit(solution)/shard_map/all_gather | solution.py:60
  57.7 2.1 fusion.22
  59.8 84.6 %all-gather.7.cloned.1.call-done = bf16[4096,512]{1,0:T(8,128)(2,1)} async-done(((bf16[64,512]{1,0:T(8,128)(2,1)}), bf16[4096,512]{1,0:T(8,128)(2,1)}) %all-gather.7.cloned.1.call-update) | async-done | bytes 4194320 | tf_op jit(solution)/shard_map/all_gather | solution.py:69
  144.4 4.1 %fusion.29 = bf16[256,512]{1,0:T(8,128)(2,1)S(1)} fusion(bf16[4096,512]{1,0:T(8,128)(2,1)} %all-gather.7.cloned.1.call-done, bf16[256,4096]{1,0:T(8,128)(2,1)} %all-gather.5.cloned.1.call-done, f32[4096]{0:T(1024)S(1)} %copy-done.1, f32[256]{0:T(256)S(1)} %add_rsqrt_fusion), kind=kOutput, calls=%fused_computation.38 | convolution fusion | flops 1078067200 | bytes 6571008 | tf_op jit(solution)/shard_map/dot_general | solution.py:67
  149.0 32.8 %while.31 = (s32[]{:T(128)}, f32[8,256]{1,0:T(8,128)S(1)}, f32[8,256]{1,0:T(8,128)S(1)}, f32[8,256,64]{1,2,0:T(8,128)S(1)}, bf16[8,256,64]{2,1,0:T(8,128)(2,1)S(...) while((s32[]{:T(128)}, f32[8,256]{1,0:T(8,128)S(1)}, ...), condition=%wide.region_10.11_spmd.clone, body=%wide.region_7.10_spmd.clone.sunk | while | flops 138415616 | bytes 6961277 | solution.py:32
  151.1 1.5 fusion.58
  155.2 1.5 fusion.58
  157.8 1.5 fusion.57
  159.3 1.5 fusion.58
  163.4 1.5 fusion.58
  167.5 1.5 fusion.58
  170.1 1.4 fusion.57
  171.6 1.5 fusion.58
  175.7 1.5 fusion.58
  178.3 1.4 fusion.57
  179.8 1.5 fusion.58
  182.6 25.2 %while.30 = (s32[]{:T(128)}, f32[8,256]{1,0:T(8,128)S(1)}, f32[8,256]{1,0:T(8,128)S(1)}, f32[8,256,64]{1,2,0:T(8,128)S(1)}, bf16[8,256,64]{2,1,0:T(8,128)(2,1)S(...) while((s32[]{:T(128)}, f32[8,256]{1,0:T(8,128)S(1)}, ...), condition=%wide.region_6.7_spmd.clone, body=%wide.region_3.6_spmd.clone.sunk | while | flops 138415616 | bytes 6961277 | solution.py:32
  183.8 1.5 fusion.55
  186.9 1.5 fusion.55
  190.1 1.5 fusion.55
  193.2 1.5 fusion.55
  196.4 1.5 fusion.55
  199.5 1.5 fusion.55
  202.7 1.5 fusion.55
  205.8 1.5 fusion.55
  209.8 19.9 %all-gather.11.cloned.1.call-done = bf16[4096,512]{1,0:T(8,128)(2,1)} async-done(((bf16[64,512]{1,0:T(8,128)(2,1)}), bf16[4096,512]{1,0:T(8,128)(2,1)}) %all-gather.11.cloned.1.call-update) | async-done | bytes 4194320 | tf_op jit(solution)/shard_map/all_gather | solution.py:85
  229.7 43.5 %all-gather.9.cloned.1.call-done = bf16[256,4096]{0,1:T(8,128)(2,1)} async-done(((bf16[256,512]{0,1:T(8,128)(2,1)}), bf16[256,4096]{0,1:T(8,128)(2,1)}) %all-gather.9.cloned.1.call-update) | async-done | bytes 2097168 | tf_op jit(solution)/shard_map/all_gather | solution.py:81
  273.1 4.8 %convolution_convert_fusion = bf16[256,512]{1,0:T(8,128)(2,1)} fusion(bf16[256,4096]{0,1:T(8,128)(2,1)} %all-gather.9.cloned.1.call-done, bf16[4096,512]{1,0:T(8,128)(2,1)} %all-gather.11.cloned.1.call-done), kind=kOutput, calls=%fused_computation.39 | convolution fusion | flops 1073872896 | bytes 6553600 | tf_op jit(solution)/shard_map/dot_general | solution.py:83
  (110 shorter events, 36.2 us)
Async XLA Ops:
  6.5 51.2 %all-gather.5.cloned.1.call-start = ((), (), s32[]{:S(2)}) async-start(), calls=%async_computation | async-start | bytes 2359296 | tf_op jit(solution)/shard_map/all_gather | solution.py:60
  7.3 137.1 %all-gather.7.cloned.1.call-start = ((), (), s32[]{:S(2)}) async-start(), calls=%async_computation.1 | async-start | bytes 4259840 | tf_op jit(solution)/shard_map/all_gather | solution.py:69
  8.0 221.6 %all-gather.11.cloned.1.call-start = ((), (), s32[]{:S(2)}) async-start(), calls=%async_computation.3 | async-start | bytes 4259840 | tf_op jit(solution)/shard_map/all_gather | solution.py:85
  11.0 8.6 %copy-start.2 = (s32[32]{0:T(128)S(1)}, s32[32]{0:T(128)}, u32[]{:S(2)}) copy-start(s32[32]{0:T(128)} %param.18) | copy-start | bytes 388
  11.0 9.8 %copy-start.3 = (s32[32]{0:T(128)S(1)}, s32[32]{0:T(128)}, u32[]{:S(2)}) copy-start(s32[32]{0:T(128)} %param.19) | copy-start | bytes 388
  11.0 137.9 %collective-permute-start = (bf16[2048,512]{0,1:T(8,128)(2,1)S(1)}, bf16[2048,512]{0,1:T(8,128)(2,1)}, u32[]{:S(2)}, u32[]{:S(2)}) collective-permute-start(bf16[2048,512]{0,1:T(8,128)(2,1)S(1)} %copy.11), channel_id=1, source_target_pairs={{0,8},{8,0},{16,24},{24,16},{32,40},{40,32},{48,56},{56,48},{64,72... | collective-permute-start | bytes 6291464 | tf_op jit(solution)/shard_map/ppermute | solution.py:12
  16.9 127.4 %copy-start.1 = (f32[4096]{0:T(1024)S(1)}, f32[4096]{0:T(1024)}, u32[]{:S(2)}) copy-start(f32[4096]{0:T(1024)} %param.13) | copy-start | bytes 49156
  16.9 132.0 %collective-permute-start.1 = (bf16[2048,512]{0,1:T(8,128)(2,1)}, bf16[2048,512]{0,1:T(8,128)(2,1)}, u32[]{:S(2)}, u32[]{:S(2)}) collective-permute-start(bf16[2048,512]{0,1:T(8,128)(2,1)} %copy.12), channel_id=1, source_target_pairs={{0,8},{8,0},{16,24},{24,16},{32,40},{40,32},{48,56},{56,48},{64,72... | collective-permute-start | bytes 6291464 | tf_op jit(solution)/shard_map/ppermute | solution.py:12
  19.5 253.7 %all-gather.9.cloned.1.call-start = ((), (), s32[]{:S(2)}) async-start(), calls=%async_computation.2 | async-start | bytes 2359296 | tf_op jit(solution)/shard_map/all_gather | solution.py:81
  181.8 0.8 copy-start
Sparse Core Ops, SparseCore 0:
  9.4 48.2 all-gather.4
  61.1 83.2 all-gather.6
  147.7 81.8 all-gather.10
  231.6 41.5 all-gather.8
where the time goes:
time: 286 us; the launch traced here: 284 us
  waiting for transfers between devices  186 us (65%)
  matrix products  48 us (17%)
  other arithmetic  22.9 us (8%)
  between operations  13.3 us (5%)
  local copies, waits for them, and re-layouts  9.49 us (3%)
  starting transfers between devices  4.57 us (2%)
    all_gather x1, waiting for transfers between devices, local(): lax.all_gather(w_query, 'ctx', axis=0, tiled=True)  84.6 us
    all_gather x1, waiting for transfers between devices, local(): all_heads = lax.all_gather(attended, 'head', axis=1, tiled=True)  43.5 us
    all_gather x1, waiting for transfers between devices, local(): full_states = lax.all_gather(dec_states, 'head', axis=1, tiled=True)  36.2 us
    dot_general x16, matrix products, one_head(): weighted = jnp.dot(weights, value_head, preferred_element_type=jnp.float32)  23.5 us
    all_gather x1, waiting for transfers between devices, local(): lax.all_gather(w_out, 'ctx', axis=0, tiled=True)  19.9 us
    dot_general x16, matrix products, one_head(): scores = jnp.dot(query_head, key_head.T, preferred_element_type=jnp.float32)  15.6 us
    unnamed x11, local copies, waits for them, and re-layouts  7.97 us
    reduce_sum x16, other arithmetic, one_head(): totals = jnp.sum(weights.astype(jnp.float32), axis=1)  6.97 us
  transfers between devices with their start and end apart: 6, of which 4 were waited for; matrix products, arithmetic and copies ran while one was open for 26% of the time, Pallas kernels for 0%

commit v1 on v0

--- a/solution.py
+++ b/solution.py
@@ -4,6 +4,13 @@
 from jax.sharding import PartitionSpec as P
 
 DK = 64
+
+
+def swapped_in(array, mesh_axis, along):
+    devices = lax.axis_size(mesh_axis)
+    blocks = jnp.stack([array for _ in range(devices)])
+    blocks = lax.all_to_all(blocks, mesh_axis, split_axis=0, concat_axis=0)
+    return jnp.concatenate(blocks, axis=along)
 
 
 def partner(value, axis, distance):
@@ -80,11 +87,7 @@
     attended = jnp.where(live_rows[:, None], attended, 0.0).astype(jnp.bfloat16)
     all_heads = lax.all_gather(attended, "head", axis=1, tiled=True)
     columns = all_heads
-    projected = jnp.dot(
-        columns,
-        lax.all_gather(w_out, "ctx", axis=0, tiled=True),
-        preferred_element_type=jnp.float32,
-    )
+    projected = jnp.dot(columns, swapped_in(w_out, "ctx", 0), preferred_element_type=jnp.float32)
     return projected.astype(jnp.bfloat16)
 
 

time: 286 us -> 277 us (0.969)
  waiting for transfers between devices: 186 us -> 156 us
  starting transfers between devices: 4.57 us -> 18.7 us
  matrix products: 48 us -> 55 us
    all_gather x1 -> x0, waiting for transfers between devices: 19.9 us -> none  [local(): lax.all_gather(w_out, 'ctx', axis=0, tiled=True)]
    all_gather x1, waiting for transfers between devices: 36.2 us -> 20 us  [local(): full_states = lax.all_gather(dec_states, 'head', axis=1, tiled=True)]
    all_to_all x0 -> x1, starting transfers between devices: none -> 14.2 us  [swapped_in(): blocks = lax.all_to_all(blocks, mesh_axis, split_axis=0, concat_axis=0)]
    all_gather x1, waiting for transfers between devices: 84.6 us -> 93.1 us  [local(): lax.all_gather(w_query, 'ctx', axis=0, tiled=True)]
    dot_general x16, matrix products: 15.6 us -> 23.1 us  [one_head(): scores = jnp.dot(query_head, key_head.T, preferred_element_type=jnp.float32)]
    unnamed x11 -> x15, local copies, waits for them, and re-layouts: 7.97 us -> 6.91 us
  transfers between devices with their start and end apart: 6 -> 6, of which waited for: 4 -> 3; matrix products, arithmetic and copies ran while one was open for 26% -> 30% of each run, Pallas kernels for 0% -> 0%
where the time goes in v1:
time: 277 us; the launch traced here: 276 us
  waiting for transfers between devices  156 us (56%)
  matrix products  55 us (20%)
  other arithmetic  21.1 us (8%)
  starting transfers between devices  18.7 us (7%)
  between operations  13.3 us (5%)
  local copies, waits for them, and re-layouts  10.9 us (4%)
    all_gather x1, waiting for transfers between devices, local(): lax.all_gather(w_query, 'ctx', axis=0, tiled=True)  93.1 us
    all_gather x1, waiting for transfers between devices, local(): all_heads = lax.all_gather(attended, 'head', axis=1, tiled=True)  41.9 us
    dot_general x16, matrix products, one_head(): weighted = jnp.dot(weights, value_head, preferred_element_type=jnp.float32)  23.5 us
    dot_general x16, matrix products, one_head(): scores = jnp.dot(query_head, key_head.T, preferred_element_type=jnp.float32)  23.1 us
    all_gather x1, waiting for transfers between devices, local(): full_states = lax.all_gather(dec_states, 'head', axis=1, tiled=True)  20 us
    all_to_all x1, starting transfers between devices, swapped_in(): blocks = lax.all_to_all(blocks, mesh_axis, split_axis=0, concat_axis=0)  14.2 us
    reduce_sum x16, other arithmetic, one_head(): totals = jnp.sum(weights.astype(jnp.float32), axis=1)  7.01 us
    unnamed x15, local copies, waits for them, and re-layouts  6.91 us
  transfers between devices with their start and end apart: 6, of which 3 were waited for; matrix products, arithmetic and copies ran while one was open for 30% of the time, Pallas kernels for 0%

profile of v1, /device:TPU:2, one launch (start us, length us, event | category | flops | bytes accessed | tf_op | source)
XLA Modules:
  0.0 276.0 jit_solution(1596267894385225841)
XLA Ops:
  8.0 4.1 %copy.12 = bf16[2048,512]{0,1:T(8,128)(2,1)} copy(bf16[2048,512]{1,0:T(8,128)(2,1)} %param.16) | data formatting | bytes 4194304 | tf_op args[4]
  12.1 2.0 collective-permute-start.1
  14.2 2.5 copy.11
  16.6 2.4 collective-permute-start
  19.1 2.5 stack.2
  21.5 14.2 %all-to-all-start = ((bf16[64,64,512]{2,1,0:T(8,128)(2,1)}), bf16[64,64,512]{2,1,0:T(8,128)(2,1)}, u32[]{:S(2)}, u32[]{:S(2)}) async-start(bf16[64,64,512]{2,1,0:T(8,128)(2,1)} %stack.2), calls=%async_computation | async-start | bytes 8388608 | tf_op jit(solution)/shard_map/all_to_all | solution.py:12
  37.7 20.0 %all-gather.4.cloned.1.call-done = bf16[256,4096]{1,0:T(8,128)(2,1)} async-done(((bf16[256,512]{1,0:T(8,128)(2,1)}), bf16[256,4096]{1,0:T(8,128)(2,1)}) %all-gather.4.cloned.1.call-update) | async-done | bytes 2097168 | tf_op jit(solution)/shard_map/all_gather | solution.py:67
  57.7 2.2 fusion.22
  59.9 93.1 %all-gather.6.cloned.1.call-done = bf16[4096,512]{1,0:T(8,128)(2,1)} async-done(((bf16[64,512]{1,0:T(8,128)(2,1)}), bf16[4096,512]{1,0:T(8,128)(2,1)}) %all-gather.6.cloned.1.call-update) | async-done | bytes 4194320 | tf_op jit(solution)/shard_map/all_gather | solution.py:76
  153.0 3.5 %fusion.29 = bf16[256,512]{1,0:T(8,128)(2,1)S(1)} fusion(bf16[4096,512]{1,0:T(8,128)(2,1)} %all-gather.6.cloned.1.call-done, bf16[256,4096]{1,0:T(8,128)(2,1)S(1)} %copy-done.1, f32[4096]{0:T(1024)S(1)} %copy-done.3, f32[256]{0:T(256)S(1)} %add_rsqrt_fusion), kind=kOutput, calls=%fused_computation.38 | convolution fusion | flops 1078067200 | bytes 6571008 | tf_op jit(solution)/shard_map/dot_general | solution.py:74
  157.1 32.3 %while.30 = (s32[]{:T(128)}, f32[8,256]{1,0:T(8,128)S(1)}, f32[8,256]{1,0:T(8,128)S(1)}, f32[8,256,64]{1,2,0:T(8,128)S(1)}, bf16[8,256,64]{2,1,0:T(8,128)(2,1)S(...) while((s32[]{:T(128)}, f32[8,256]{1,0:T(8,128)S(1)}, ...), condition=%wide.region_6.7_spmd.clone, body=%wide.region_3.6_spmd.clone.sunk | while | flops 138415616 | bytes 6961285 | solution.py:39
  159.6 1.5 fusion.55
  163.6 1.5 fusion.55
  167.6 1.5 fusion.55
  171.7 1.5 fusion.55
  175.7 1.5 fusion.55
  179.8 1.5 fusion.55
  183.8 1.5 fusion.55
  187.9 1.5 fusion.55
  189.5 32.3 %while.31 = (s32[]{:T(128)}, f32[8,256]{1,0:T(8,128)S(1)}, f32[8,256]{1,0:T(8,128)S(1)}, f32[8,256,64]{1,2,0:T(8,128)S(1)}, bf16[8,256,64]{2,1,0:T(8,128)(2,1)S(...) while((s32[]{:T(128)}, f32[8,256]{1,0:T(8,128)S(1)}, ...), condition=%wide.region_10.11_spmd.clone, body=%wide.region_7.10_spmd.clone.sunk | while | flops 138415616 | bytes 6961285 | solution.py:39
  192.0 1.5 fusion.58
  196.0 1.5 fusion.58
  200.1 1.5 fusion.58
  202.2 1.4 fusion.57
  204.1 1.5 fusion.58
  206.3 1.4 fusion.57
  208.2 1.5 fusion.58
  212.2 1.5 fusion.58
  216.2 1.5 fusion.58
  220.3 1.5 fusion.58
  222.8 41.9 %all-gather.8.cloned.1.call-done = bf16[256,4096]{0,1:T(8,128)(2,1)} async-done(((bf16[256,512]{0,1:T(8,128)(2,1)}), bf16[256,4096]{0,1:T(8,128)(2,1)}) %all-gather.8.cloned.1.call-update) | async-done | bytes 2097168 | tf_op jit(solution)/shard_map/all_gather | solution.py:88
  264.7 4.8 %convolution_convert_fusion = bf16[256,512]{1,0:T(8,128)(2,1)} fusion(bf16[256,4096]{0,1:T(8,128)(2,1)} %all-gather.8.cloned.1.call-done, bf16[4096,512]{1,0:T(8,128)(2,1)} %bitcast.18), kind=kOutput, calls=%fused_computation.39 | convolution fusion | flops 1073872896 | bytes 6553600 | tf_op jit(solution)/shard_map/dot_general | solution.py:90
  (114 shorter events, 42.5 us)
Async XLA Ops:
  6.5 51.1 %all-gather.4.cloned.1.call-start = ((), (), s32[]{:S(2)}) async-start(), calls=%async_computation.1 | async-start | bytes 2359296 | tf_op jit(solution)/shard_map/all_gather | solution.py:67
  7.3 145.8 %all-gather.6.cloned.1.call-start = ((), (), s32[]{:S(2)}) async-start(), calls=%async_computation.2 | async-start | bytes 4259840 | tf_op jit(solution)/shard_map/all_gather | solution.py:76
  8.0 6.2 %copy-start = (bf16[2048,512]{1,0:T(8,128)(2,1)S(1)}, bf16[2048,512]{1,0:T(8,128)(2,1)}, u32[]{:S(2)}) copy-start(bf16[2048,512]{1,0:T(8,128)(2,1)} %param.15) | copy-start | bytes 6291460
  12.1 6.9 %copy-start.2 = (bf16[64,512]{1,0:T(8,128)(2,1)S(1)}, bf16[64,512]{1,0:T(8,128)(2,1)}, u32[]{:S(2)}) copy-start(bf16[64,512]{1,0:T(8,128)(2,1)} %param.17) | copy-start | bytes 196612
  12.1 177.3 %collective-permute-start.1 = (bf16[2048,512]{0,1:T(8,128)(2,1)}, bf16[2048,512]{0,1:T(8,128)(2,1)}, u32[]{:S(2)}, u32[]{:S(2)}) collective-permute-start(bf16[2048,512]{0,1:T(8,128)(2,1)} %copy.12), channel_id=1, source_target_pairs={{0,8},{8,0},{16,24},{24,16},{32,40},{40,32},{48,56},{56,48},{64,72... | collective-permute-start | bytes 6291464 | tf_op jit(solution)/shard_map/ppermute | solution.py:19
  16.6 172.8 %collective-permute-start = (bf16[2048,512]{0,1:T(8,128)(2,1)}, bf16[2048,512]{0,1:T(8,128)(2,1)}, u32[]{:S(2)}, u32[]{:S(2)}) collective-permute-start(bf16[2048,512]{0,1:T(8,128)(2,1)} %copy.11), channel_id=1, source_target_pairs={{0,8},{8,0},{16,24},{24,16},{32,40},{40,32},{48,56},{56,48},{64,72... | collective-permute-start | bytes 6291464 | tf_op jit(solution)/shard_map/ppermute | solution.py:19
  21.5 14.3 %copy-start.4 = (s32[32]{0:T(128)S(1)}, s32[32]{0:T(128)}, u32[]{:S(2)}) copy-start(s32[32]{0:T(128)} %param.18) | copy-start | bytes 388
  21.5 15.5 %copy-start.5 = (s32[32]{0:T(128)S(1)}, s32[32]{0:T(128)}, u32[]{:S(2)}) copy-start(s32[32]{0:T(128)} %param.19) | copy-start | bytes 388
  21.5 201.2 %all-to-all-start = ((bf16[64,64,512]{2,1,0:T(8,128)(2,1)}), bf16[64,64,512]{2,1,0:T(8,128)(2,1)}, u32[]{:S(2)}, u32[]{:S(2)}) async-start(bf16[64,64,512]{2,1,0:T(8,128)(2,1)} %stack.2), calls=%async_computation | async-start | bytes 8388608 | tf_op jit(solution)/shard_map/all_to_all | solution.py:12
  35.7 117.3 %copy-start.3 = (f32[4096]{0:T(1024)S(1)}, f32[4096]{0:T(1024)}, u32[]{:S(2)}) copy-start(f32[4096]{0:T(1024)} %param.13) | copy-start | bytes 49156
  35.7 229.0 %all-gather.8.cloned.1.call-start = ((), (), s32[]{:S(2)}) async-start(), calls=%async_computation.3 | async-start | bytes 2359296 | tf_op jit(solution)/shard_map/all_gather | solution.py:88
  57.7 95.4 %copy-start.1 = (bf16[256,4096]{1,0:T(8,128)(2,1)S(1)}, bf16[256,4096]{1,0:T(8,128)(2,1)}, u32[]{:S(2)}) copy-start(bf16[256,4096]{1,0:T(8,128)(2,1)} %all-gather.4.cloned.1.call-done) | copy-start | bytes 6291460
Sparse Core Ops, SparseCore 0:
  9.4 48.1 all-gather.3
  61.0 91.9 all-gather.5
  222.9 41.7 all-gather.7
